TPU v7x, 256 devices: a whole 4x4x8 slice. The times are simulated.
256 devices in a mesh: tm: 32 (over y, z), space: 8 (over x, core).
Axes of the slice: x: 4, y: 4, z: 8, core: 2. Of those that a mesh axis runs over, the one named last changes fastest.
Arguments:
- inverse_factor: bfloat16 [2, 32, 4096, 4096], P(None, 'tm', 'space'), may hold values from -1.5 to 1.5, as said below
- tile_mask: int32 [32, 32], replicated, may hold values 0 or 1
- carry_rate: float32 [32, 4096, 2], P('tm', 'space'), may hold values from 0 to 1
- right_side: float32 [32, 4096, 2, 128], P('tm', 'space'), may hold values from -1.5 to 1.5
- arrow_rows: bfloat16 [32, 4096, 2, 512], P('tm', 'space'), may hold values from -0.0625 to 0.0625
- fixed_rhs: float32 [2, 512, 128], P(None, ('tm', 'space')), may hold values from -6 to 6
- tip_factor: bfloat16 [2, 512, 512], replicated, may hold values from -1 to 1, as said below
Outputs:
- solution: float32 [32, 4096, 2, 128], P('tm', 'space')
- fixed_solution: float32 [2, 512, 128], P(None, ('tm', 'space'))
Inputs may be any that keep to these rules, and one draw needn't show every extreme that they name: `tile_mask`: 1 marks a tile that may be nonzero. `inverse_factor`: only entries on or below the diagonal are read. `tip_factor`: only entries on or below the diagonal are read.
All inputs are finite; a program needn't handle non-finite values.
Results may differ from a plain program's by a relative error of at most 0.022.
Values may be sent and summed in bfloat16 or wider, within the bound.
No kernel may reach another device: no remote copies, remote signals or barrier semaphores. Data moves between devices by JAX's collectives and lax.ppermute only.
A program may use at most 320 MiB of HBM per device.

v0:
```python
import jax
import jax.numpy as jnp
from jax import lax
from jax.sharding import PartitionSpec as P

TILE = 128


def carried_in(shard, axis, join, neutral, backward):
    count = lax.axis_size(axis)
    place = lax.axis_index(axis)
    ahead = count - 1 - place if backward else place
    gathered = jax.tree.map(
        lambda a, kind: lax.all_gather(a.astype(kind), axis), shard, (jnp.bfloat16, jnp.bfloat16)
    )
    state = jax.tree.map(lambda a, e: jnp.zeros_like(a) + jnp.asarray(e, a.dtype), shard, neutral)

    def one(turn, state):
        source = count - 1 - turn if backward else turn
        return join(
            state,
            jax.tree.map(
                lambda a, own: lax.dynamic_index_in_dim(a, source, 0, False).astype(own.dtype),
                gathered,
                shard,
            ),
        )

    return lax.fori_loop(0, ahead, one, state)


def combine(earlier, latter):
    rate_new = latter[0] * earlier[0]
    rest = tuple(
        (value_l + latter[0] * value_e for value_l, value_e in zip(latter[1:], earlier[1:]))
    )
    return (rate_new,) + rest


def tile_keep(tile_table, row_start, row_total, col_total):
    tile_count = tile_table.shape[0]
    tile_ids = jnp.arange(tile_count, dtype=jnp.int32)
    row_index = row_start + jnp.arange(row_total, dtype=jnp.int32)
    col_index = jnp.arange(col_total, dtype=jnp.int32)
    row_onehot = (row_index[:, None] // TILE == tile_ids[None, :]).astype(jnp.float32)
    col_onehot = (col_index[:, None] // TILE == tile_ids[None, :]).astype(jnp.float32)
    marked = jnp.dot(jnp.dot(row_onehot, tile_table.astype(jnp.float32)), col_onehot.T)
    return (marked > 0.5) & (row_index[:, None] >= col_index[None, :])


def on_device(inverse_factor, tile_mask, carry_rate, right_side, arrow_rows, fixed_rhs, tip_factor):
    row_count = right_side.shape[1]
    node_total = inverse_factor.shape[3]
    row_start = lax.axis_index("space") * row_count
    tile_table = jnp.maximum(tile_mask, jnp.eye(tile_mask.shape[0], dtype=jnp.int32))
    weights = inverse_factor[:, 0]
    bf_zero = jnp.zeros((), jnp.bfloat16)
    rate_col = carry_rate[0][:, :, None]
    source = right_side[0]
    unit_rate = jnp.ones_like(rate_col)
    earlier_sum = carried_in(
        (rate_col, source), "tm", combine, (unit_rate, jnp.zeros_like(source)), False
    )
    forward = source + rate_col * earlier_sum[1]
    forward_b = forward.astype(jnp.bfloat16)
    row_keep = tile_keep(tile_table, row_start, row_count, node_total)
    masked_rows = jnp.where(row_keep[None], weights, bf_zero)
    block = masked_rows
    inner_rows = jnp.einsum(
        "hrn,nhk->rhk",
        block,
        lax.all_gather(forward_b, "space", axis=0, tiled=True),
        preferred_element_type=jnp.float32,
    ).astype(jnp.bfloat16)
    block = masked_rows
    scaled = lax.psum_scatter(
        jnp.einsum("hrn,rhk->nhk", block, inner_rows, preferred_element_type=jnp.float32).astype(
            jnp.bfloat16
        ),
        "space",
        scatter_dimension=0,
        tiled=True,
    ).astype(jnp.float32)
    arrow_part = arrow_rows[0]
    coupling = jnp.einsum("rhf,rhk->hfk", arrow_part, forward_b, preferred_element_type=jnp.float32)
    share_rows = fixed_rhs.shape[1]
    share_start = lax.axis_index(("tm", "space")) * share_rows
    contrib = -coupling
    own_part = lax.dynamic_slice_in_dim(contrib, share_start, share_rows, 1) + fixed_rhs
    contrib = lax.dynamic_update_slice_in_dim(contrib, own_part, share_start, 1)
    fixed_forward = lax.psum(contrib, ("tm", "space")).astype(jnp.bfloat16)
    fixed_total = tip_factor.shape[1]
    fixed_index = jnp.arange(fixed_total, dtype=jnp.int32)
    lower_tri = fixed_index[:, None] >= fixed_index[None, :]
    tip_lower = jnp.where(lower_tri[None], tip_factor, bf_zero)
    tip_inner = jnp.einsum(
        "hij,hjk->hik", tip_lower, fixed_forward, preferred_element_type=jnp.float32
    ).astype(jnp.bfloat16)
    fixed_solution = jnp.einsum(
        "hij,hik->hjk", tip_lower, tip_inner, preferred_element_type=jnp.float32
    )
    fixed_own = lax.dynamic_slice_in_dim(fixed_solution, share_start, share_rows, 1)
    fixed_b = fixed_solution.astype(jnp.bfloat16)
    carried = scaled - jnp.einsum(
        "rhf,hfk->rhk", arrow_part, fixed_b, preferred_element_type=jnp.float32
    )
    following = carried_in(
        (rate_col, rate_col * carried), "tm", combine, (unit_rate, jnp.zeros_like(carried)), True
    )
    solution = carried + following[1]
    return (solution[None], fixed_own)


def solution(mesh):
    placed = (
        P(None, "tm", "space", None),
        P(),
        P("tm", "space", None),
        P("tm", "space", None, None),
        P("tm", "space", None, None),
        P(None, ("tm", "space"), None),
        P(),
    )
    return jax.shard_map(
        on_device,
        mesh=mesh,
        in_specs=placed,
        out_specs=(P("tm", "space", None, None), P(None, ("tm", "space"), None)),
        check_vma=False,
    )
```

profile of v0, /device:TPU:2, one launch (start us, length us, event | category | flops | bytes accessed | tf_op | source)
XLA Modules:
  0.0 596.0 jit_solution(12626880782622736189)
XLA Ops:
  11.1 52.1 %all-gather = bf16[32,512,2]{1,2,0:T(2,128)(2,1)S(1)} all-gather(bf16[1,512,2]{1,2,0:T(2,128)(2,1)S(1)} %convert_element_type.103), channel_id=2, replica_groups=mesh['tm'=32,'space'=8] {'tm'}, dimensions={0}, use_global_device_ids=true | all-gather | bytes 67584 | tf_op jit(solution)/shard_map/all_gather | solution.py:14
  63.2 3.3 copy.37
  66.6 46.1 %all-gather.6.cloned.1.call-done = bf16[32,512,2,128]{3,1,2,0:T(8,128)(2,1)} async-done(((bf16[1,512,2,128]{3,1,2,0:T(8,128)(2,1)}), bf16[32,512,2,128]{3,1,2,0:T(8,128)(2,1)}) %all-gather.6.cloned.1.call-update) | async-done | bytes 8388624 | tf_op jit(solution)/shard_map/all_gather | solution.py:14
  114.4 4.2 fusion
  118.6 154.2 %all-gather.8.cloned.1.call-done = bf16[4096,2,128]{0,2,1:T(8,128)(2,1)} async-done(((bf16[512,2,128]{0,2,1:T(8,128)(2,1)}), bf16[4096,2,128]{0,2,1:T(8,128)(2,1)}) %all-gather.8.cloned.1.call-update) | async-done | bytes 2097168 | tf_op jit(solution)/shard_map/all_gather | solution.py:72
  272.7 13.2 %fusion.4 = bf16[4096,2,128]{0,2,1:T(8,128)(2,1)} fusion(bf16[2,1,512,4096]{3,2,1,0:T(8,128)(2,1)} %param.11, pred[512,4096]{1,0:T(8,128)(4,1)} %fusion, bf16[4096,2,128]{0,2,1:T(8,128)(2,1)} %all-gather.8.cloned.1.call-done), kind=kOutput, calls=%fused_computation.12 | convolution fusion | flops 2157051904 | bytes 14680064 | tf_op jit(solution)/shard_map/hrn,rhk->nhk/dot_general | solution.py:77
  287.8 78.9 %all-reduce.1 = bf16[2,512,128]{1,2,0:T(8,128)(2,1)S(1)} all-reduce(f32[2,512,128]{1,2,0:T(8,128)S(1)} %dynamic_update_slice.3), channel_id=1, replica_groups=mesh['tm'=32,'space'=8] {'tm','space'}, use_global_device_ids=true, to_apply=%region_3.4 | all-reduce | flops 131072 | bytes 786432 | tf_op jit(solution)/shard_map/psum | solution.py:91
  366.7 2.3 fusion.9
  369.0 2.1 multiply_convert_fusion
  371.8 102.9 %all-gather.10.cloned.1.call-done = bf16[16384,2,128]{0,2,1:T(8,128)(2,1)} async-done(((bf16[512,2,128]{0,2,1:T(8,128)(2,1)}), bf16[16384,2,128]{0,2,1:T(8,128)(2,1)}) %all-gather.10.cloned.1.call-update) | async-done | bytes 8388624 | tf_op jit(solution)/shard_map/all_gather | solution.py:14
  474.7 21.1 %copy.52 = bf16[16384,2,128]{2,1,0:T(2,128)(2,1)} copy(bf16[16384,2,128]{0,2,1:T(8,128)(2,1)} %all-gather.10.cloned.1.call-done) | data formatting | bytes 16777216 | tf_op jit(solution)/shard_map/while | solution.py:29
  495.9 92.2 %while.27 = (s32[]{:T(128)}, f32[512,2,128]{2,1,0:T(2,128)S(1)}, s32[]{:T(128)}, bf16[32,512,2,128]{3,2,1,0:T(2,128)(2,1)}, bf16[32,512,2,1]{2,1,3,0:T(8,128)(2,...) while((s32[]{:T(128)}, f32[512,2,128]{2,1,0:T(2,128)S(1)}, s32[]{:T(128)}, ...), condition=%wide.region_5.6_spmd, body=%wide.region_4.5_spmd.sunk | while | flops 394246 | bytes 1321107 | solution.py:29
  499.8 2.0 convert_add_fusion.5
  502.8 2.0 convert_add_fusion.5
  505.8 2.0 convert_add_fusion.5
  508.8 2.0 convert_add_fusion.5
  511.7 2.0 convert_add_fusion.5
  520.7 2.0 convert_add_fusion.5
  523.6 2.0 convert_add_fusion.5
  526.6 2.0 convert_add_fusion.5
  529.6 2.0 convert_add_fusion.5
  538.5 2.0 convert_add_fusion.5
  541.5 2.0 convert_add_fusion.5
  544.5 2.0 convert_add_fusion.5
  547.4 2.0 convert_add_fusion.5
  556.3 2.0 convert_add_fusion.5
  559.3 2.0 convert_add_fusion.5
  562.3 2.0 convert_add_fusion.5
  565.3 2.0 convert_add_fusion.5
  568.2 2.0 convert_add_fusion.5
  577.2 2.0 convert_add_fusion.5
  580.1 2.0 convert_add_fusion.5
  (80 shorter events, 60.3 us)
Async XLA Ops:
  7.2 279.1 %copy-start = (bf16[1,512,2,512]{3,2,1,0:T(2,128)(2,1)S(1)}, bf16[1,512,2,512]{3,2,1,0:T(2,128)(2,1)}, u32[]{:S(2)}) copy-start(bf16[1,512,2,512]{3,2,1,0:T(2,128)(2,1)} %param.15) | copy-start | bytes 3145732
  7.2 105.5 %all-gather.6.cloned.1.call-start = ((), (), s32[]{:S(2)}) async-start(), calls=%async_computation.1 | async-start | bytes 8650752 | tf_op jit(solution)/shard_map/all_gather | solution.py:14
  9.1 263.6 %all-gather.8.cloned.1.call-start = ((), (), s32[]{:S(2)}) async-start(), calls=%async_computation.2 | async-start | bytes 2359296 | tf_op jit(solution)/shard_map/all_gather | solution.py:72
  112.8 0.7 copy-start.2
  112.8 1.6 copy-start.4
  114.3 254.7 %reduce-scatter.2.cloned.1.call-start = ((), (), s32[]{:S(2)}) async-start(), calls=%async_computation.3 | async-start | bytes 2359296 | tf_op jit(solution)/shard_map/reduce_scatter | solution.py:76
  118.6 167.5 %copy-start.3 = (f32[2,2,128]{2,1,0:T(2,128)S(1)}, f32[2,2,128]{2,1,0:T(2,128)}, u32[]{:S(2)}) copy-start(f32[2,2,128]{2,1,0:T(2,128)} %param.16) | copy-start | bytes 6148
  118.6 167.7 %copy-start.1 = (bf16[512,2,128]{0,2,1:T(8,128)(2,1)S(1)}, bf16[512,2,128]{0,2,1:T(8,128)(2,1)}, u32[]{:S(2)}) copy-start(bf16[512,2,128]{0,2,1:T(8,128)(2,1)} %fusion.19) | copy-start | bytes 786436
  286.0 188.7 %all-gather.10.cloned.1.call-start = ((), (), s32[]{:S(2)}) async-start(), calls=%async_computation.4 | async-start | bytes 8650752 | tf_op jit(solution)/shard_map/all_gather | solution.py:14
Sparse Core Ops, SparseCore 0:
  11.2 101.4 all-gather.5
  115.0 157.6 all-gather.7
  286.1 34.6 reduce-scatter.1
  371.3 103.2 all-gather.9
where the time goes:
time: 598 us; the launch traced here: 596 us
  waiting for transfers between devices  303 us (51%)
  blocking collectives  131 us (22%)
  other arithmetic  92.9 us (16%)
  local copies, waits for them, and re-layouts  31.4 us (5%)
  matrix products  22.2 us (4%)
  between operations  14 us (2%)
    all_gather x1, waiting for transfers between devices, on_device(): lax.all_gather(forward_b, 'space', axis=0, tiled=True)  154 us
    all_gather x2, waiting for transfers between devices, carried_in(): lax.all_gather(a.astype(kind), axis)  149 us
    psum x1, blocking collectives, on_device(): fixed_forward = lax.psum(contrib, ('tm', 'space')).astype(jnp.bfloat16)  78.9 us
    add x31, other arithmetic, combine(): value_l + latter[0] * value_e  62.3 us
    all_gather x1, blocking collectives, carried_in(): lax.all_gather(a.astype(kind), axis)  52.1 us
    convert_element_type x31, other arithmetic, one(): lax.dynamic_index_in_dim(a, source, 0, False).astype(own.dtype)  28.8 us
    while x4, local copies, waits for them, and re-layouts, carried_in(): return lax.fori_loop(0, ahead, one, state)  24.8 us
    dot_general x1, matrix products, on_device(): jnp.einsum('hrn,rhk->nhk', block, inner_rows, preferred_element_type=jnp....  13.2 us
  transfers between devices with their start and end apart: 4, of which 3 were waited for; matrix products, arithmetic and copies ran while one was open for 2% of the time, Pallas kernels for 0%

commit v1 on v0

--- a/solution.py
+++ b/solution.py
@@ -4,6 +4,18 @@
 from jax.sharding import PartitionSpec as P
 
 TILE = 128
+
+
+def summed_around(shard, axis, dim, term):
+    size, place = (lax.axis_size(axis), lax.axis_index(axis))
+    downward = [(i, (i - 1) % size) for i in range(size)]
+    extent = shard.shape[dim]
+    held = shard
+    so_far = term(held, place * extent)
+    for step in range(1, size):
+        held = lax.ppermute(held, axis, downward)
+        so_far = so_far + term(held, (place + step) % size * extent)
+    return so_far
 
 
 def carried_in(shard, axis, join, neutral, backward):
@@ -66,11 +78,16 @@
     row_keep = tile_keep(tile_table, row_start, row_count, node_total)
     masked_rows = jnp.where(row_keep[None], weights, bf_zero)
     block = masked_rows
-    inner_rows = jnp.einsum(
-        "hrn,nhk->rhk",
-        block,
-        lax.all_gather(forward_b, "space", axis=0, tiled=True),
-        preferred_element_type=jnp.float32,
+    inner_rows = summed_around(
+        forward_b,
+        "space",
+        0,
+        lambda own_block, offset: jnp.einsum(
+            "hrn,nhk->rhk",
+            lax.dynamic_slice_in_dim(block, offset, own_block.shape[0], axis=2),
+            own_block,
+            preferred_element_type=jnp.float32,
+        ),
     ).astype(jnp.bfloat16)
     block = masked_rows
     scaled = lax.psum_scatter(

time: 598 us -> 616 us (1.030)
  waiting for transfers between devices: 303 us -> 157 us
  blocking collectives: 131 us -> 269 us
  starting transfers between devices: 0.16 us -> 13.1 us
  other arithmetic: 92.9 us -> 101 us
    all_gather x1 -> x0, waiting for transfers between devices: 154 us -> none  [on_device(): lax.all_gather(forward_b, 'space', axis=0, tiled=True)]
    psum x1, blocking collectives: 78.9 us -> 217 us  [on_device(): fixed_forward = lax.psum(contrib, ('tm', 'space')).astype(jnp.bfloat16)]
    ppermute x0 -> x7, starting transfers between devices: none -> 13 us  [summed_around(): held = lax.ppermute(held, axis, downward)]
    dot_general x0 -> x7, matrix products: none -> 11.9 us  [on_device(): jnp.einsum('hrn,nhk->rhk', lax.dynamic_slice_in_dim(block, offset, own_bl...]
    ppermute x0 -> x7, waiting for transfers between devices: none -> 9.17 us  [summed_around(): held = lax.ppermute(held, axis, downward)]
    select_n x0 -> x1, other arithmetic: none -> 8.49 us  [on_device(): masked_rows = jnp.where(row_keep[None], weights, bf_zero)]
    dot_general x1, matrix products: 13.2 us -> 6.72 us  [on_device(): jnp.einsum('hrn,rhk->nhk', block, inner_rows, preferred_element_type=jnp....]
  transfers between devices with their start and end apart: 4 -> 10, of which waited for: 3 -> 7; matrix products, arithmetic and copies ran while one was open for 2% -> 6% of each run, Pallas kernels for 0% -> 0%
where the time goes in v1:
time: 616 us; the launch traced here: 613 us
  blocking collectives  269 us (44%)
  waiting for transfers between devices  157 us (25%)
  other arithmetic  101 us (16%)
  local copies, waits for them, and re-layouts  31.1 us (5%)
  matrix products  27.5 us (4%)
  between operations  14 us (2%)
  starting transfers between devices  13.1 us (2%)
    psum x1, blocking collectives, on_device(): fixed_forward = lax.psum(contrib, ('tm', 'space')).astype(jnp.bfloat16)  217 us
    all_gather x2, waiting for transfers between devices, carried_in(): lax.all_gather(a.astype(kind), axis)  148 us
    add x31, other arithmetic, combine(): value_l + latter[0] * value_e  62.3 us
    all_gather x1, blocking collectives, carried_in(): lax.all_gather(a.astype(kind), axis)  52.1 us
    convert_element_type x31, other arithmetic, one(): lax.dynamic_index_in_dim(a, source, 0, False).astype(own.dtype)  28.7 us
    while x4, local copies, waits for them, and re-layouts, carried_in(): return lax.fori_loop(0, ahead, one, state)  24.9 us
    ppermute x7, starting transfers between devices, summed_around(): held = lax.ppermute(held, axis, downward)  13 us
  transfers between devices with their start and end apart: 10, of which 7 were waited for; matrix products, arithmetic and copies ran while one was open for 6% of the time, Pallas kernels for 0%

profile of v1, /device:TPU:2, one launch (start us, length us, event | category | flops | bytes accessed | tf_op | source)
XLA Modules:
  0.0 613.1 jit_solution(5150134408606604293)
XLA Ops:
  11.1 52.1 %all-gather = bf16[32,512,2]{1,2,0:T(2,128)(2,1)S(1)} all-gather(bf16[1,512,2]{1,2,0:T(2,128)(2,1)S(1)} %convert_element_type.100), channel_id=2, replica_groups=mesh['tm'=32,'space'=8] {'tm'}, dimensions={0}, use_global_device_ids=true | all-gather | bytes 67584 | tf_op jit(solution)/shard_map/all_gather | solution.py:26
  63.2 3.3 copy.37
  66.6 46.1 %all-gather.5.cloned.1.call-done = bf16[32,512,2,128]{3,1,2,0:T(8,128)(2,1)} async-done(((bf16[1,512,2,128]{3,1,2,0:T(8,128)(2,1)}), bf16[32,512,2,128]{3,1,2,0:T(8,128)(2,1)}) %all-gather.5.cloned.1.call-update) | async-done | bytes 8388624 | tf_op jit(solution)/shard_map/all_gather | solution.py:26
  113.2 3.9 collective-permute-done
  119.0 3.9 collective-permute-done.1
  124.8 4.1 fusion
  130.6 8.5 %bitcast_select_fusion = bf16[2,512,4096]{2,1,0:T(8,128)(2,1)} fusion(bf16[2,1,512,4096]{3,2,1,0:T(8,128)(2,1)} %param.11, pred[512,4096]{1,0:T(8,128)(4,1)} %fusion), kind=kLoop, calls=%fused_computation.6 | loop fusion | flops 4194304 | bytes 18874368 | tf_op jit(solution)/shard_map/jit(_where)/select_n | solution.py:79
  140.8 3.1 collective-permute-start.4
  147.8 2.4 collective-permute-start.5
  159.9 6.7 %fusion.1 = bf16[4096,2,128]{0,2,1:T(8,128)(2,1)} fusion(bf16[2,512,4096]{2,1,0:T(8,128)(2,1)} %bitcast_select_fusion, f32[2,128,512]{2,1,0:T(8,128)S(1)} %convolution_add_fusion.1, bf16[512,2,128]{0,2,1:T(8,128)(2,1)S(1)} %collective-permute-done.6, s32[]{:T(128)S(6)} %select_n.122), kind=kOutput, calls=%fused_computation.10 | convolution fusion | flops 1209270272 | bytes 12320772 | tf_op jit(solution)/shard_map/hrn,rhk->nhk/dot_general | solution.py:94
  168.5 216.5 %all-reduce.1 = bf16[2,512,128]{1,2,0:T(8,128)(2,1)S(1)} all-reduce(f32[2,512,128]{1,2,0:T(8,128)S(1)} %dynamic_update_slice.3), channel_id=1, replica_groups=mesh['tm'=32,'space'=8] {'tm','space'}, use_global_device_ids=true, to_apply=%region_3.4 | all-reduce | flops 131072 | bytes 786432 | tf_op jit(solution)/shard_map/psum | solution.py:108
  385.0 2.3 fusion.4
  387.3 2.1 multiply_convert_fusion
  390.1 101.9 %all-gather.7.cloned.1.call-done = bf16[16384,2,128]{0,2,1:T(8,128)(2,1)} async-done(((bf16[512,2,128]{0,2,1:T(8,128)(2,1)}), bf16[16384,2,128]{0,2,1:T(8,128)(2,1)}) %all-gather.7.cloned.1.call-update) | async-done | bytes 8388624 | tf_op jit(solution)/shard_map/all_gather | solution.py:26
  492.0 21.1 %copy.52 = bf16[16384,2,128]{2,1,0:T(2,128)(2,1)} copy(bf16[16384,2,128]{0,2,1:T(8,128)(2,1)} %all-gather.7.cloned.1.call-done) | data formatting | bytes 16777216 | tf_op jit(solution)/shard_map/while | solution.py:41
  513.2 92.0 %while.27 = (s32[]{:T(128)}, f32[512,2,128]{2,1,0:T(2,128)S(1)}, s32[]{:T(128)}, bf16[32,512,2,128]{3,2,1,0:T(2,128)(2,1)}, bf16[32,512,2,1]{2,1,3,0:T(8,128)(2,...) while((s32[]{:T(128)}, f32[512,2,128]{2,1,0:T(2,128)S(1)}, s32[]{:T(128)}, ...), condition=%wide.region_5.6_spmd, body=%wide.region_4.5_spmd.sunk | while | flops 394246 | bytes 1321115 | solution.py:41
  514.2 2.0 convert_add_fusion.5
  517.1 2.0 convert_add_fusion.5
  520.1 2.0 convert_add_fusion.5
  523.1 2.0 convert_add_fusion.5
  526.0 2.0 convert_add_fusion.5
  529.0 2.0 convert_add_fusion.5
  532.0 2.0 convert_add_fusion.5
  534.9 2.0 convert_add_fusion.5
  555.7 2.0 convert_add_fusion.5
  558.7 2.0 convert_add_fusion.5
  561.7 2.0 convert_add_fusion.5
  564.6 2.0 convert_add_fusion.5
  567.6 2.0 convert_add_fusion.5
  570.6 2.0 convert_add_fusion.5
  573.5 2.0 convert_add_fusion.5
  576.5 2.0 convert_add_fusion.5
  (97 shorter events, 87.8 us)
Async XLA Ops:
  7.2 159.8 %copy-start = (bf16[1,512,2,512]{3,2,1,0:T(2,128)(2,1)S(1)}, bf16[1,512,2,512]{3,2,1,0:T(2,128)(2,1)}, u32[]{:S(2)}) copy-start(bf16[1,512,2,512]{3,2,1,0:T(2,128)(2,1)} %param.15) | copy-start | bytes 3145732
  7.2 105.5 %all-gather.5.cloned.1.call-start = ((), (), s32[]{:S(2)}) async-start(), calls=%async_computation.1 | async-start | bytes 8650752 | tf_op jit(solution)/shard_map/all_gather | solution.py:26
  9.1 378.2 %reduce-scatter.2.cloned.1.call-start = ((), (), s32[]{:S(2)}) async-start(), calls=%async_computation.2 | async-start | bytes 2359296 | tf_op jit(solution)/shard_map/reduce_scatter | solution.py:93
  63.2 49.8 %copy-start.1 = (f32[1,512,2]{1,2,0:T(2,128)S(1)}, f32[1,512,2]{1,2,0:T(2,128)}, u32[]{:S(2)}) copy-start(f32[1,512,2]{1,2,0:T(2,128)} %param.13) | copy-start | bytes 12292
  66.6 58.2 %copy-start.3 = (s32[32,32]{1,0:T(8,128)S(1)}, s32[32,32]{1,0:T(8,128)}, u32[]{:S(2)}) copy-start(s32[32,32]{1,0:T(8,128)} %param.12) | copy-start | bytes 12292
  113.1 3.9 collective-permute-start
  117.0 5.8 collective-permute-start.1
  122.8 6.0 collective-permute-start.2
  128.9 11.9 %collective-permute-start.3 = (bf16[512,2,128]{0,2,1:T(8,128)(2,1)S(1)}, bf16[512,2,128]{0,2,1:T(8,128)(2,1)S(1)}, u32[]{:S(2)}, u32[]{:S(2)}) collective-permute-start(bf16[512,2,128]{0,2,1:T(8,128)(2,1)S(1)} %collective-permute-done.2), channel_id=1, source_target_pairs={{0,7},{1,0},{2,1},{3,2},{4,3},{5,4},{6,5},{7,6},{8,15},{9,8},{10,9... | collective-permute-start | bytes 786440 | tf_op jit(solution)/shard_map/ppermute | solution.py:16
  140.8 7.0 %collective-permute-start.4 = (bf16[512,2,128]{0,2,1:T(8,128)(2,1)S(1)}, bf16[512,2,128]{0,2,1:T(8,128)(2,1)S(1)}, u32[]{:S(2)}, u32[]{:S(2)}) collective-permute-start(bf16[512,2,128]{0,2,1:T(8,128)(2,1)S(1)} %collective-permute-done.3), channel_id=1, source_target_pairs={{0,7},{1,0},{2,1},{3,2},{4,3},{5,4},{6,5},{7,6},{8,15},{9,8},{10,9... | collective-permute-start | bytes 786440 | tf_op jit(solution)/shard_map/ppermute | solution.py:16
  147.8 6.3 %collective-permute-start.5 = (bf16[512,2,128]{0,2,1:T(8,128)(2,1)S(1)}, bf16[512,2,128]{0,2,1:T(8,128)(2,1)S(1)}, u32[]{:S(2)}, u32[]{:S(2)}) collective-permute-start(bf16[512,2,128]{0,2,1:T(8,128)(2,1)S(1)} %collective-permute-done.4), channel_id=1, source_target_pairs={{0,7},{1,0},{2,1},{3,2},{4,3},{5,4},{6,5},{7,6},{8,15},{9,8},{10,9... | collective-permute-start | bytes 786440 | tf_op jit(solution)/shard_map/ppermute | solution.py:16
  154.1 5.8 collective-permute-start.6
  157.7 9.0 %copy-start.2 = (f32[2,2,128]{2,1,0:T(2,128)S(1)}, f32[2,2,128]{2,1,0:T(2,128)}, u32[]{:S(2)}) copy-start(f32[2,2,128]{2,1,0:T(2,128)} %param.16) | copy-start | bytes 6148
  166.7 325.3 %all-gather.7.cloned.1.call-start = ((), (), s32[]{:S(2)}) async-start(), calls=%async_computation.3 | async-start | bytes 8650752 | tf_op jit(solution)/shard_map/all_gather | solution.py:26
Sparse Core Ops, SparseCore 0:
  11.2 101.4 all-gather.4
  166.8 169.4 reduce-scatter.1
  389.6 102.2 all-gather.6
